TPU v7x, 32 devices: a whole 2x2x4 slice. The times are simulated.
32 devices in a mesh: groups: 2 (over y), points: 4 (over z), centers: 4 (over x, core).
Axes of the slice: x: 2, y: 2, z: 4, core: 2. Of those that a mesh axis runs over, the one named last changes fastest.
Arguments:
- train_points: bfloat16 [8192, 512], P(('groups', 'points')), parts along dimension 0, may hold values from -6 to 6
- saved_preds: float32 [8192, 128], P(('groups', 'points')), parts along dimension 0, may hold values from -6 to 6
- targets: float32 [8192, 128], P(('groups', 'points')), parts along dimension 0, may hold values from -6 to 6
- huber_delta: float32 [256], P('groups'), parts along dimension 0, may hold values from 0.3 to 3
- center_pos: bfloat16 [16384, 512], P(('groups', 'points', 'centers')), parts along dimension 0, may hold values from -6 to 6
- coefficients: bfloat16 [16384, 128], P(('groups', 'points', 'centers')), parts along dimension 0, may hold values from -0.8984375 to 0.8984375
- spread: bfloat16 [16384], P(('groups', 'points', 'centers')), parts along dimension 0, may hold values from 0.5 to 2
Outputs:
- grad_centers: float32 [16384, 512], P(('groups', 'points', 'centers')), parts along dimension 0
- grad_coef: float32 [16384, 128], P(('groups', 'points', 'centers')), parts along dimension 0
There are 2 independent parts, one for each index of `groups`. A program takes and returns all parts, laid end to end along the dimension named above; each array names one. Nothing has to cross between parts.
All inputs are finite; a program needn't handle non-finite values.
Results may differ from a plain program's by a relative error of at most 0.0003.
Values may be sent and summed in bfloat16 or wider, within the bound.
No kernel may reach another device: no remote copies, remote signals or barrier semaphores. Data moves between devices by JAX's collectives and lax.ppermute only.
A program may use at most 64 MiB of HBM per device.

v0:
```python
import jax
import jax.numpy as jnp
from jax import lax
from jax.sharding import PartitionSpec as P


def per_device(train_points, saved_preds, targets, huber_delta, center_pos, coefficients, spread):
    n_points, in_width = train_points.shape
    whole_pos, whole_coef, whole_rates = (
        lax.all_gather(center_pos, "points", axis=0, tiled=True),
        lax.all_gather(coefficients, "points", axis=0, tiled=True),
        lax.all_gather(spread, "points", axis=0, tiled=True),
    )
    center_sq = jnp.sum(jnp.square(whole_pos.astype(jnp.float32)), axis=1)
    rates = whole_rates.astype(jnp.float32)
    panel_width = whole_pos.shape[0]
    out_width = whole_coef.shape[1]
    block_rows = min(512, n_points)
    block_count = n_points // block_rows
    point_blocks = train_points.reshape(block_count, block_rows, in_width)

    def kernel_of(row_block):
        point_sq = jnp.sum(jnp.square(row_block.astype(jnp.float32)), axis=1)
        cross = lax.dot_general(
            row_block, whole_pos, (((1,), (1,)), ((), ())), preferred_element_type=jnp.float32
        )
        dist = point_sq[:, None] + center_sq[None, :] - 2.0 * cross
        return jnp.exp(-rates[None, :] * dist / in_width).astype(jnp.bfloat16)

    kernels = lax.map(kernel_of, point_blocks)
    partial_pred = jnp.dot(
        kernels.reshape(n_points, panel_width), whole_coef, preferred_element_type=jnp.float32
    )
    panel_pred = lax.psum(partial_pred, "centers")
    residual = panel_pred + saved_preds - targets
    cotangent = (residual / jnp.sqrt(1.0 + jnp.square(residual / huber_delta[None, :]))).astype(
        jnp.bfloat16
    )
    cot_blocks = cotangent.reshape(block_count, block_rows, out_width)

    def coef_term(kernel, cot_block):
        return lax.dot_general(
            kernel, cot_block, (((0,), (0,)), ((), ())), preferred_element_type=jnp.float32
        )

    def moment_terms(kernel, cot_block, row_block):
        mixing = lax.dot_general(
            cot_block, whole_coef, (((1,), (1,)), ((), ())), preferred_element_type=jnp.float32
        )
        weights = (kernel.astype(jnp.float32) * mixing).astype(jnp.bfloat16)
        totals = jnp.sum(weights.astype(jnp.float32), axis=0)
        moment = lax.dot_general(
            weights, row_block, (((0,), (0,)), ((), ())), preferred_element_type=jnp.float32
        )
        return (moment, totals)

    zero_coef = jnp.zeros((panel_width, out_width), jnp.float32)
    zero_moment = jnp.zeros((panel_width, in_width), jnp.float32)
    zero_totals = jnp.zeros((panel_width,), jnp.float32)

    def coef_pass(coef_acc, inputs):
        row_block, stored, cot_block = inputs
        return (coef_acc + coef_term(stored, cot_block), None)

    coef_acc, _ = lax.scan(coef_pass, zero_coef, (point_blocks, kernels, cot_blocks))
    grad_coef = lax.psum_scatter(coef_acc, "points", scatter_dimension=0, tiled=True)

    def moment_pass(totals, inputs):
        moment_acc, totals_acc = totals
        row_block, stored, cot_block = inputs
        moment, row_sum = moment_terms(stored, cot_block, row_block)
        return ((moment_acc + moment, totals_acc + row_sum), None)

    (moment_acc, totals_acc), _ = lax.scan(
        moment_pass, (zero_moment, zero_totals), (point_blocks, kernels, cot_blocks)
    )
    own_moment, own_totals = (
        lax.psum_scatter(moment_acc, "points", scatter_dimension=0, tiled=True),
        lax.psum_scatter(totals_acc, "points", scatter_dimension=0, tiled=True),
    )
    own_rates = spread.astype(jnp.float32)
    grad_centers = (2.0 * own_rates / in_width)[:, None] * (
        own_moment - own_totals[:, None] * center_pos.astype(jnp.float32)
    )
    return (grad_centers, grad_coef)


def solution(mesh):
    return jax.shard_map(
        per_device,
        mesh=mesh,
        in_specs=(
            P(("groups", "points"), None),
            P(("groups", "points"), None),
            P(("groups", "points"), None),
            P("groups"),
            P(("groups", "points", "centers"), None),
            P(("groups", "points", "centers"), None),
            P(("groups", "points", "centers")),
        ),
        out_specs=(
            P(("groups", "points", "centers"), None),
            P(("groups", "points", "centers"), None),
        ),
        check_vma=False,
    )
```

profile of v0, /device:TPU:0, one launch (start us, length us, event | category | flops | bytes accessed | tf_op | source)
XLA Modules:
  0.0 246.5 jit_solution(6114186068954046954)
XLA Ops:
  7.2 0.0 all-gather.3.cloned.1.call-start
  7.2 0.7 all-gather.3.cloned.1.call-update
  7.9 0.0 all-reduce.3.cloned.1.call-start
  8.0 0.7 reshape.29
  8.6 13.5 %all-gather = bf16[4,1,512]{2,1,0:T(2,128)(2,1)S(1)} all-gather(bf16[1,1,512]{2,1,0:T(2,128)(2,1)S(1)} %reshape.29), channel_id=1, replica_groups=mesh['groups'=2,'points'=4,'centers'=4] {'points'}, dimensions={0}, use_global_device_ids=true | all-gather | bytes 5120 | tf_op jit(solution)/shard_map/all_gather | solution.py:12
  22.2 22.0 %all_gather.11 = bf16[2048,128]{1,0:T(8,128)(2,1)} all-gather(bf16[512,128]{1,0:T(8,128)(2,1)} %param.18), channel_id=1, replica_groups=mesh['groups'=2,'points'=4,'centers'=4] {'points'}, dimensions={0}, use_global_device_ids=true | all-gather | bytes 655360 | tf_op jit(solution)/shard_map/all_gather | solution.py:11
  44.2 22.4 %all-gather.3.cloned.1.call-done = bf16[2048,512]{1,0:T(8,128)(2,1)} async-done(((bf16[512,512]{1,0:T(8,128)(2,1)}), bf16[2048,512]{1,0:T(8,128)(2,1)}) %all-gather.3.cloned.1.call-update) | async-done | bytes 2097168 | tf_op jit(solution)/shard_map/all_gather | solution.py:10
  66.5 2.1 multiply_reduce_fusion.1
  68.6 11.9 %while.36 = (s32[]{:T(128)}, bf16[2,512,2048]{2,1,0:T(8,128)(2,1)}, f32[1,2048]{1,0:T(1,128)S(1)}, bf16[2,512,512]{2,1,0:T(8,128)(2,1)}, f32[2048]{0:T(1024)S(1)}, /*index=5*/bf16[2048,512]{1,0:T(8,128)(2,1)}, s32[]{:T(128)}) while((s32[]{:T(128)}, bf16[2,512,2048]{2,1,0:T(8,128)(2,1)}, f32[1,2048]{1,0:T(1,128)S(1)}, ...), condition=%wide.region_3.4_spmd, body=%wide.region_1.3_spmd.sunk | while | flops 1080819200 | bytes 5264465 | solution.py:30
  68.6 1.2 multiply_reduce_fusion.3
  69.8 4.7 %fusion.33 = bf16[2,512,2048]{2,1,0:T(8,128)(2,1)} fusion(bf16[2,512,2048]{2,1,0:T(8,128)(2,1)} %get-tuple-element.330, s32[]{:T(128)} %get-tuple-element.329, bf16[2048,512]{1,0:T(8,128)(2,1)} %get-tuple-element.341, f32[2048]{0:T(1024)S(1)} %get-tuple-element.340, f32[512]{0:T(512)S(1)} %multiply_reduce_fusion.3, f32[2048]{0:T(1024)S(1)} %bitcast.62, ...), kind=kOutput, calls=%fused_computation.2.clone.1 | convolution fusion | flops 1080033280 | bytes 4738048 | tf_op jit(solution)/shard_map/while/body/eval_jaxpr/dot_general | solution.py:24
  74.5 1.2 multiply_reduce_fusion.3
  75.7 4.7 %fusion.33 = bf16[2,512,2048]{2,1,0:T(8,128)(2,1)} fusion(bf16[2,512,2048]{2,1,0:T(8,128)(2,1)} %get-tuple-element.330, s32[]{:T(128)} %get-tuple-element.329, bf16[2048,512]{1,0:T(8,128)(2,1)} %get-tuple-element.341, f32[2048]{0:T(1024)S(1)} %get-tuple-element.340, f32[512]{0:T(512)S(1)} %multiply_reduce_fusion.3, f32[2048]{0:T(1024)S(1)} %bitcast.62, ...), kind=kOutput, calls=%fused_computation.2.clone.1 | convolution fusion | flops 1080033280 | bytes 4738048 | tf_op jit(solution)/shard_map/while/body/eval_jaxpr/dot_general | solution.py:24
  80.5 0.0 copy-start.3
  80.5 0.0 copy-start.4
  80.5 0.0 copy-start.6
  80.5 0.0 copy-start.1
  80.5 4.5 %fusion.17 = f32[1024,128]{1,0:T(8,128)} fusion(bf16[1024,2048]{1,0:T(8,128)(2,1)} %bitcast.58, bf16[2048,128]{1,0:T(8,128)(2,1)} %all_gather.11), kind=kOutput, calls=%fused_computation.29 | convolution fusion | flops 536870912 | bytes 5242880 | tf_op jit(solution)/shard_map/dot_general | solution.py:31
  85.0 0.0 all-reduce.3.cloned.1.call-update
  85.0 0.0 reduce-scatter.3.cloned.1.call-start
  85.1 32.1 %all-reduce.3.cloned.1.call-done = f32[1024,128]{1,0:T(8,128)} async-done(((f32[1024,128]{1,0:T(8,128)}), f32[1024,128]{1,0:T(8,128)}) %all-reduce.3.cloned.1.call-update) | async-done | bytes 524304 | tf_op jit(solution)/shard_map/psum | solution.py:34
  117.1 0.0 copy-done.3
  117.1 0.0 copy-done.4
  117.1 0.0 copy-done.6
  117.1 1.2 multiply_convert_fusion
  118.3 0.0 copy-done.1
  118.3 13.7 %while.37 = (s32[]{:T(128)}, f32[2048,512]{1,0:T(8,128)}, f32[2048]{0:T(1024)S(1)}, bf16[2,512,2048]{2,1,0:T(8,128)(2,1)}, bf16[2,512,128]{2,1,0:T(8,128)(2,1)S(...) while((s32[]{:T(128)}, f32[2048,512]{1,0:T(8,128)}, ...), condition=%wide.region_7.8_spmd.clone, body=%wide.region_5.7_spmd.clone.sunk | while | flops 1349519360 | bytes 15893612 | solution.py:74
  118.3 2.5 %convert_reduce_fusion.2 = (f32[2048]{0:T(1024)S(1)}, bf16[512,2048]{1,0:T(8,128)(2,1)S(1)}) fusion(bf16[2048,128]{1,0:T(8,128)(2,1)} %get-tuple-element.366, bf16[2,512,128]{2,1,0:T(8,128)(2,1)S(1)} %get-tuple-element.365, s32[]{:T(128)} %get-tuple-element.352, bf16[2,512,2048]{2,1,0:T(8,128)(2,1)} %get-tuple-element.364), kind=kOutput, calls=%fused_computation.10.clone.1 | convolution fusion | flops 273676288 | bytes 4858880 | tf_op jit(solution)/shard_map/while/body/eval_jaxpr/dot_general | solution.py:47
  120.8 3.2 %select_add_fusion.4 = f32[2048,512]{1,0:T(8,128)} fusion(f32[2048,512]{1,0:T(8,128)} %get-tuple-element.353, bf16[512,2048]{1,0:T(8,128)(2,1)S(1)} %get-tuple-element.316, pred[]{:T(512)S(6)} %compare.6, bf16[2,512,512]{2,1,0:T(8,128)(2,1)S(1)} %get-tuple-element.367, s32[]{:T(128)} %get-tuple-element.352), kind=kOutput, calls=%fused_computation.9.clone.1 | convolution fusion | flops 1075838976 | bytes 11010053 | tf_op jit(solution)/shard_map/while/body/eval_jaxpr/dot_general | solution.py:52
  124.1 2.5 %convert_reduce_fusion.2 = (f32[2048]{0:T(1024)S(1)}, bf16[512,2048]{1,0:T(8,128)(2,1)S(1)}) fusion(bf16[2048,128]{1,0:T(8,128)(2,1)} %get-tuple-element.366, bf16[2,512,128]{2,1,0:T(8,128)(2,1)S(1)} %get-tuple-element.365, s32[]{:T(128)} %get-tuple-element.352, bf16[2,512,2048]{2,1,0:T(8,128)(2,1)} %get-tuple-element.364), kind=kOutput, calls=%fused_computation.10.clone.1 | convolution fusion | flops 273676288 | bytes 4858880 | tf_op jit(solution)/shard_map/while/body/eval_jaxpr/dot_general | solution.py:47
  126.6 5.4 %select_add_fusion.4 = f32[2048,512]{1,0:T(8,128)} fusion(f32[2048,512]{1,0:T(8,128)} %get-tuple-element.353, bf16[512,2048]{1,0:T(8,128)(2,1)S(1)} %get-tuple-element.316, pred[]{:T(512)S(6)} %compare.6, bf16[2,512,512]{2,1,0:T(8,128)(2,1)S(1)} %get-tuple-element.367, s32[]{:T(128)} %get-tuple-element.352), kind=kOutput, calls=%fused_computation.9.clone.1 | convolution fusion | flops 1075838976 | bytes 11010053 | tf_op jit(solution)/shard_map/while/body/eval_jaxpr/dot_general | solution.py:52
  132.0 0.0 reduce-scatter.3.cloned.1.call-update
  132.1 0.0 reduce-scatter.5.cloned.1.call-start
  132.1 0.0 copy-start.7
  132.1 0.0 copy-start.5
  132.1 0.0 copy-start.2
  132.2 5.4 %while.38 = (s32[]{:T(128)}, f32[2048,128]{1,0:T(8,128)S(1)}, bf16[2,512,2048]{2,1,0:T(8,128)(2,1)}, bf16[2,512,128]{2,1,0:T(8,128)(2,1)S(1)}, s32[]{:T(128)}, /*index=5*/s32[]{:T(128)}) while((s32[]{:T(128)}, f32[2048,128]{1,0:T(8,128)S(1)}, bf16[2,512,2048]{2,1,0:T(8,128)(2,1)}, bf16[2,512,128]{2,1,0:T(8,128)(2,1)S(1)}, ...), condition=%wide.region_11.12_spmd.clone, body=%wide.region_10.11_spmd.clone.sunk | while | flops 268959744 | bytes 4326479 | solution.py:65
  132.2 2.7 %convolution_add_fusion.2 = f32[2048,128]{1,0:T(8,128)S(1)} fusion(bf16[2,512,2048]{2,1,0:T(8,128)(2,1)} %get-tuple-element.384, s32[]{:T(128)} %get-tuple-element.376, f32[2048,128]{1,0:T(8,128)S(1)} %get-tuple-element.377, pred[]{:T(512)S(6)} %compare.7, bf16[2,512,128]{2,1,0:T(8,128)(2,1)S(1)} %get-tuple-element.385), kind=kOutput, calls=%fused_computation.18.clone.1 | convolution fusion | flops 268959744 | bytes 4326401 | tf_op jit(solution)/shard_map/while/body/eval_jaxpr/dot_general | solution.py:42
  134.9 2.6 %convolution_add_fusion.2 = f32[2048,128]{1,0:T(8,128)S(1)} fusion(bf16[2,512,2048]{2,1,0:T(8,128)(2,1)} %get-tuple-element.384, s32[]{:T(128)} %get-tuple-element.376, f32[2048,128]{1,0:T(8,128)S(1)} %get-tuple-element.377, pred[]{:T(512)S(6)} %compare.7, bf16[2,512,128]{2,1,0:T(8,128)(2,1)S(1)} %get-tuple-element.385), kind=kOutput, calls=%fused_computation.18.clone.1 | convolution fusion | flops 268959744 | bytes 4326401 | tf_op jit(solution)/shard_map/while/body/eval_jaxpr/dot_general | solution.py:42
  137.5 0.0 copy-start
  137.6 1.0 copy-done
  138.5 0.0 reduce-scatter.5.cloned.1.call-update
  138.5 0.0 copy-done.7
  138.6 0.6 dynamic-slice
  139.8 0.0 copy-done.5
  139.8 12.4 %all-reduce = f32[2048]{0:T(1024)S(1)} all-reduce(f32[2048]{0:T(1024)S(1)} %get-tuple-element.136), channel_id=3, replica_groups=mesh['groups'=2,'points'=4,'centers'=4] {'points'}, use_global_device_ids=true, to_apply=%region_9.10.clone | all-reduce | flops 2048 | bytes 16384
  152.2 0.1 dynamic-slice.1
  152.3 57.2 %reduce-scatter.3.cloned.1.call-done = f32[512,512]{1,0:T(8,128)} async-done(((f32[2048,512]{1,0:T(8,128)}), f32[512,512]{1,0:T(8,128)}) %reduce-scatter.3.cloned.1.call-update) | async-done | bytes 1048592 | tf_op jit(solution)/shard_map/reduce_scatter | solution.py:78
  209.5 0.0 copy-done.2
  209.5 2.4 subtract_multiply_fusion
  211.9 28.1 %reduce-scatter.5.cloned.1.call-done = f32[512,128]{1,0:T(8,128)} async-done(((f32[2048,128]{1,0:T(8,128)}), f32[512,128]{1,0:T(8,128)}) %reduce-scatter.5.cloned.1.call-update) | async-done | bytes 262160 | tf_op jit(solution)/shard_map/reduce_scatter | solution.py:66
  (8 shorter events, 0.0 us)
Async XLA Ops:
  7.2 59.4 %all-gather.3.cloned.1.call-start = ((), (), s32[]{:S(2)}) async-start(), calls=%async_computation.2 | async-start | bytes 2621440 | tf_op jit(solution)/shard_map/all_gather | solution.py:10
  7.9 109.2 %all-reduce.3.cloned.1.call-start = ((), (), s32[]{:S(2)}) async-start(), calls=%async_computation.3 | async-start | bytes 1048576 | tf_op jit(solution)/shard_map/psum | solution.py:34
  80.5 36.7 %copy-start.3 = (f32[1024,128]{1,0:T(8,128)S(1)}, f32[1024,128]{1,0:T(8,128)}, u32[]{:S(2)}) copy-start(f32[1024,128]{1,0:T(8,128)} %param.15) | copy-start | bytes 1572868
  80.5 36.7 %copy-start.4 = (f32[1024,128]{1,0:T(8,128)S(1)}, f32[1024,128]{1,0:T(8,128)}, u32[]{:S(2)}) copy-start(f32[1024,128]{1,0:T(8,128)} %param.14) | copy-start | bytes 1572868
  80.5 36.7 %copy-start.6 = (f32[128]{0:T(128)S(1)}, f32[128]{0:T(128)}, u32[]{:S(2)}) copy-start(f32[128]{0:T(128)} %param.16) | copy-start | bytes 1540
  80.5 37.8 %copy-start.1 = (bf16[2,512,512]{2,1,0:T(8,128)(2,1)S(1)}, bf16[2,512,512]{2,1,0:T(8,128)(2,1)}, u32[]{:S(2)}) copy-start(bf16[2,512,512]{2,1,0:T(8,128)(2,1)} %get-tuple-element.397) | copy-start | bytes 3145732
  85.0 124.5 %reduce-scatter.3.cloned.1.call-start = ((), (), s32[]{:S(2)}) async-start(), calls=%async_computation.4 | async-start | bytes 5242880 | tf_op jit(solution)/shard_map/reduce_scatter | solution.py:78
  132.1 108.0 %reduce-scatter.5.cloned.1.call-start = ((), (), s32[]{:S(2)}) async-start(), calls=%async_computation.5 | async-start | bytes 1310720 | tf_op jit(solution)/shard_map/reduce_scatter | solution.py:66
  132.1 6.4 %copy-start.7 = (u32[32]{0:T(128)S(1)}, u32[32]{0:T(128)}, u32[]{:S(2)}) copy-start(u32[32]{0:T(128)} %constant.66) | copy-start | bytes 388
  132.1 7.7 %copy-start.5 = (bf16[512]{0:T(512)(128)(2,1)S(1)}, bf16[512]{0:T(512)(128)(2,1)}, u32[]{:S(2)}) copy-start(bf16[512]{0:T(512)(128)(2,1)} %param.19) | copy-start | bytes 3076
  132.1 77.4 %copy-start.2 = (bf16[512,512]{1,0:T(8,128)(2,1)S(1)}, bf16[512,512]{1,0:T(8,128)(2,1)}, u32[]{:S(2)}) copy-start(bf16[512,512]{1,0:T(8,128)(2,1)} %param.17) | copy-start | bytes 1572868
  137.5 1.0 copy-start
Sparse Core Ops, SparseCore 0:
  9.6 56.9 all-gather.2
  85.1 31.9 all-reduce.2
  132.2 77.2 reduce-scatter.2
  212.3 27.6 reduce-scatter.4
where the time goes:
time: 247 us
  waiting for transfers between devices  140 us (57%)
  blocking collectives  47.9 us (19%)
  matrix products  32.9 us (13%)
  between operations  14.6 us (6%)
  other arithmetic  8.14 us (3%)
    reduce_scatter x1, waiting for transfers between devices, per_device(): lax.psum_scatter(moment_acc, 'points', scatter_dimension=0, tiled=True)  57.2 us
    psum x1, waiting for transfers between devices, per_device(): panel_pred = lax.psum(partial_pred, 'centers')  32.1 us
    reduce_scatter x1, waiting for transfers between devices, per_device(): lax.psum_scatter(coef_acc, 'points', scatter_dimension=0, tiled=True)  28.1 us
    all_gather x1, waiting for transfers between devices, per_device(): lax.all_gather(center_pos, 'points', axis=0, tiled=True)  22.4 us
    all_gather x1, blocking collectives, per_device(): lax.all_gather(coefficients, 'points', axis=0, tiled=True)  22 us
    all_gather x1, blocking collectives, per_device(): lax.all_gather(spread, 'points', axis=0, tiled=True)  13.5 us
    unnamed x1, blocking collectives  12.4 us
    dot_general x2, matrix products, kernel_of(): lax.dot_general(row_block, whole_pos, (((1,), (1,)), ((), ())), preferred...  9.42 us
  transfers between devices with their start and end apart: 4, of which 4 were waited for; matrix products, arithmetic and copies ran while one was open for 4% of the time, Pallas kernels for 0%

commit v1 on v0

--- a/solution.py
+++ b/solution.py
@@ -2,6 +2,12 @@
 import jax.numpy as jnp
 from jax import lax
 from jax.sharding import PartitionSpec as P
+from jax.lax import all_gather
+
+
+def group_load(block_in, row_axis):
+    field_out = all_gather(block_in, axis_name=row_axis)
+    return jnp.sum(field_out, 0)
 
 
 def per_device(train_points, saved_preds, targets, huber_delta, center_pos, coefficients, spread):
@@ -31,7 +37,7 @@
     partial_pred = jnp.dot(
         kernels.reshape(n_points, panel_width), whole_coef, preferred_element_type=jnp.float32
     )
-    panel_pred = lax.psum(partial_pred, "centers")
+    panel_pred = group_load(partial_pred, "centers")
     residual = panel_pred + saved_preds - targets
     cotangent = (residual / jnp.sqrt(1.0 + jnp.square(residual / huber_delta[None, :]))).astype(
         jnp.bfloat16

time: 247 us -> 237 us (0.960)
  waiting for transfers between devices: 140 us -> 130 us
    psum x1 -> x0, waiting for transfers between devices: 32.1 us -> none  [per_device(): panel_pred = lax.psum(partial_pred, 'centers')]
    all_gather x0 -> x1, waiting for transfers between devices: none -> 21.4 us  [group_load(): field_out = all_gather(block_in, axis_name=row_axis)]
where the time goes in v1:
time: 237 us
  waiting for transfers between devices  130 us (55%)
  blocking collectives  47.8 us (20%)
  matrix products  32.9 us (14%)
  between operations  14.6 us (6%)
  other arithmetic  8.86 us (4%)
    reduce_scatter x1, waiting for transfers between devices, per_device(): lax.psum_scatter(moment_acc, 'points', scatter_dimension=0, tiled=True)  57.3 us
    reduce_scatter x1, waiting for transfers between devices, per_device(): lax.psum_scatter(coef_acc, 'points', scatter_dimension=0, tiled=True)  28.1 us
    all_gather x1, waiting for transfers between devices, per_device(): lax.all_gather(center_pos, 'points', axis=0, tiled=True)  22.4 us
    all_gather x1, blocking collectives, per_device(): lax.all_gather(coefficients, 'points', axis=0, tiled=True)  22 us
    all_gather x1, waiting for transfers between devices, group_load(): field_out = all_gather(block_in, axis_name=row_axis)  21.4 us
    all_gather x1, blocking collectives, per_device(): lax.all_gather(spread, 'points', axis=0, tiled=True)  13.5 us
    unnamed x1, blocking collectives  12.3 us
    dot_general x2, matrix products, kernel_of(): lax.dot_general(row_block, whole_pos, (((1,), (1,)), ((), ())), preferred...  9.42 us
  transfers between devices with their start and end apart: 4, of which 4 were waited for; matrix products, arithmetic and copies ran while one was open for 4% of the time, Pallas kernels for 0%

profile of v1, /device:TPU:0, one launch (start us, length us, event | category | flops | bytes accessed | tf_op | source)
XLA Modules:
  0.0 236.7 jit_solution(12979579379665027416)
XLA Ops:
  7.2 0.0 all-gather.5.cloned.1.call-start
  7.2 0.7 all-gather.5.cloned.1.call-update
  7.9 0.0 all-gather.7.cloned.1.call-start
  8.0 0.7 reshape.30
  8.6 13.5 %all-gather.1 = bf16[4,1,512]{2,1,0:T(2,128)(2,1)S(1)} all-gather(bf16[1,1,512]{2,1,0:T(2,128)(2,1)S(1)} %reshape.30), channel_id=1, replica_groups=mesh['groups'=2,'points'=4,'centers'=4] {'points'}, dimensions={0}, use_global_device_ids=true | all-gather | bytes 5120 | tf_op jit(solution)/shard_map/all_gather | solution.py:18
  22.2 22.0 %all_gather.17 = bf16[2048,128]{1,0:T(8,128)(2,1)} all-gather(bf16[512,128]{1,0:T(8,128)(2,1)} %param.18), channel_id=1, replica_groups=mesh['groups'=2,'points'=4,'centers'=4] {'points'}, dimensions={0}, use_global_device_ids=true | all-gather | bytes 655360 | tf_op jit(solution)/shard_map/all_gather | solution.py:17
  44.2 22.4 %all-gather.5.cloned.1.call-done = bf16[2048,512]{1,0:T(8,128)(2,1)} async-done(((bf16[512,512]{1,0:T(8,128)(2,1)}), bf16[2048,512]{1,0:T(8,128)(2,1)}) %all-gather.5.cloned.1.call-update) | async-done | bytes 2097168 | tf_op jit(solution)/shard_map/all_gather | solution.py:16
  66.5 2.1 multiply_reduce_fusion.1
  68.6 11.9 %while.36 = (s32[]{:T(128)}, bf16[2,512,2048]{2,1,0:T(8,128)(2,1)}, f32[1,2048]{1,0:T(1,128)S(1)}, bf16[2,512,512]{2,1,0:T(8,128)(2,1)}, f32[2048]{0:T(1024)S(1)}, /*index=5*/bf16[2048,512]{1,0:T(8,128)(2,1)}, s32[]{:T(128)}) while((s32[]{:T(128)}, bf16[2,512,2048]{2,1,0:T(8,128)(2,1)}, f32[1,2048]{1,0:T(1,128)S(1)}, ...), condition=%wide.region_3.4_spmd, body=%wide.region_1.3_spmd.sunk | while | flops 1080819200 | bytes 5264465 | solution.py:36
  68.6 1.2 multiply_reduce_fusion.3
  69.8 4.7 %fusion.33 = bf16[2,512,2048]{2,1,0:T(8,128)(2,1)} fusion(bf16[2,512,2048]{2,1,0:T(8,128)(2,1)} %get-tuple-element.330, s32[]{:T(128)} %get-tuple-element.329, bf16[2048,512]{1,0:T(8,128)(2,1)} %get-tuple-element.341, f32[2048]{0:T(1024)S(1)} %get-tuple-element.340, f32[512]{0:T(512)S(1)} %multiply_reduce_fusion.3, f32[2048]{0:T(1024)S(1)} %bitcast.64, ...), kind=kOutput, calls=%fused_computation.2.clone.1 | convolution fusion | flops 1080033280 | bytes 4738048 | tf_op jit(solution)/shard_map/while/body/eval_jaxpr/dot_general | solution.py:30
  74.5 1.2 multiply_reduce_fusion.3
  75.7 4.7 %fusion.33 = bf16[2,512,2048]{2,1,0:T(8,128)(2,1)} fusion(bf16[2,512,2048]{2,1,0:T(8,128)(2,1)} %get-tuple-element.330, s32[]{:T(128)} %get-tuple-element.329, bf16[2048,512]{1,0:T(8,128)(2,1)} %get-tuple-element.341, f32[2048]{0:T(1024)S(1)} %get-tuple-element.340, f32[512]{0:T(512)S(1)} %multiply_reduce_fusion.3, f32[2048]{0:T(1024)S(1)} %bitcast.64, ...), kind=kOutput, calls=%fused_computation.2.clone.1 | convolution fusion | flops 1080033280 | bytes 4738048 | tf_op jit(solution)/shard_map/while/body/eval_jaxpr/dot_general | solution.py:30
  80.5 0.0 copy-start.3
  80.5 0.0 copy-start.4
  80.5 0.0 copy-start.6
  80.5 0.0 copy-start.1
  80.5 4.5 %fusion.17 = f32[1024,128]{1,0:T(8,128)} fusion(bf16[1024,2048]{1,0:T(8,128)(2,1)} %bitcast.59, bf16[2048,128]{1,0:T(8,128)(2,1)} %all_gather.17), kind=kOutput, calls=%fused_computation.29 | convolution fusion | flops 536870912 | bytes 5242880 | tf_op jit(solution)/shard_map/dot_general | solution.py:37
  85.0 0.0 all-gather.7.cloned.1.call-update
  85.0 0.0 reduce-scatter.3.cloned.1.call-start
  85.1 21.4 %all-gather.7.cloned.1.call-done = f32[4096,128]{1,0:T(8,128)} async-done(((f32[1024,128]{1,0:T(8,128)}), f32[4096,128]{1,0:T(8,128)}) %all-gather.7.cloned.1.call-update) | async-done | bytes 2097168 | tf_op jit(solution)/shard_map/all_gather | solution.py:9
  106.5 1.8 reduce_sum.39
  108.3 0.0 copy-done.3
  108.3 0.0 copy-done.4
  108.3 0.0 copy-done.6
  108.3 0.2 multiply_convert_fusion
  108.5 0.0 copy-done.1
  108.5 13.7 %while.37 = (s32[]{:T(128)}, f32[2048,512]{1,0:T(8,128)}, f32[2048]{0:T(1024)S(1)}, bf16[2,512,2048]{2,1,0:T(8,128)(2,1)}, bf16[2,512,128]{2,1,0:T(8,128)(2,1)S(...) while((s32[]{:T(128)}, f32[2048,512]{1,0:T(8,128)}, ...), condition=%wide.region_7.8_spmd.clone, body=%wide.region_5.7_spmd.clone.sunk | while | flops 1349519360 | bytes 15893612 | solution.py:80
  108.5 2.5 %convert_reduce_fusion.2 = (f32[2048]{0:T(1024)S(1)}, bf16[512,2048]{1,0:T(8,128)(2,1)S(1)}) fusion(bf16[2048,128]{1,0:T(8,128)(2,1)} %get-tuple-element.366, bf16[2,512,128]{2,1,0:T(8,128)(2,1)S(1)} %get-tuple-element.365, s32[]{:T(128)} %get-tuple-element.352, bf16[2,512,2048]{2,1,0:T(8,128)(2,1)} %get-tuple-element.364), kind=kOutput, calls=%fused_computation.10.clone.1 | convolution fusion | flops 273676288 | bytes 4858880 | tf_op jit(solution)/shard_map/while/body/eval_jaxpr/dot_general | solution.py:53
  111.0 3.2 %select_add_fusion.4 = f32[2048,512]{1,0:T(8,128)} fusion(f32[2048,512]{1,0:T(8,128)} %get-tuple-element.353, bf16[512,2048]{1,0:T(8,128)(2,1)S(1)} %get-tuple-element.316, pred[]{:T(512)S(6)} %compare.6, bf16[2,512,512]{2,1,0:T(8,128)(2,1)S(1)} %get-tuple-element.367, s32[]{:T(128)} %get-tuple-element.352), kind=kOutput, calls=%fused_computation.9.clone.1 | convolution fusion | flops 1075838976 | bytes 11010053 | tf_op jit(solution)/shard_map/while/body/eval_jaxpr/dot_general | solution.py:58
  114.2 2.5 %convert_reduce_fusion.2 = (f32[2048]{0:T(1024)S(1)}, bf16[512,2048]{1,0:T(8,128)(2,1)S(1)}) fusion(bf16[2048,128]{1,0:T(8,128)(2,1)} %get-tuple-element.366, bf16[2,512,128]{2,1,0:T(8,128)(2,1)S(1)} %get-tuple-element.365, s32[]{:T(128)} %get-tuple-element.352, bf16[2,512,2048]{2,1,0:T(8,128)(2,1)} %get-tuple-element.364), kind=kOutput, calls=%fused_computation.10.clone.1 | convolution fusion | flops 273676288 | bytes 4858880 | tf_op jit(solution)/shard_map/while/body/eval_jaxpr/dot_general | solution.py:53
  116.7 5.4 %select_add_fusion.4 = f32[2048,512]{1,0:T(8,128)} fusion(f32[2048,512]{1,0:T(8,128)} %get-tuple-element.353, bf16[512,2048]{1,0:T(8,128)(2,1)S(1)} %get-tuple-element.316, pred[]{:T(512)S(6)} %compare.6, bf16[2,512,512]{2,1,0:T(8,128)(2,1)S(1)} %get-tuple-element.367, s32[]{:T(128)} %get-tuple-element.352), kind=kOutput, calls=%fused_computation.9.clone.1 | convolution fusion | flops 1075838976 | bytes 11010053 | tf_op jit(solution)/shard_map/while/body/eval_jaxpr/dot_general | solution.py:58
  122.2 0.0 reduce-scatter.3.cloned.1.call-update
  122.2 0.0 reduce-scatter.5.cloned.1.call-start
  122.3 0.0 copy-start.7
  122.3 0.0 copy-start.5
  122.3 0.0 copy-start.2
  122.3 5.4 %while.38 = (s32[]{:T(128)}, f32[2048,128]{1,0:T(8,128)S(1)}, bf16[2,512,2048]{2,1,0:T(8,128)(2,1)}, bf16[2,512,128]{2,1,0:T(8,128)(2,1)S(1)}, s32[]{:T(128)}, /*index=5*/s32[]{:T(128)}) while((s32[]{:T(128)}, f32[2048,128]{1,0:T(8,128)S(1)}, bf16[2,512,2048]{2,1,0:T(8,128)(2,1)}, bf16[2,512,128]{2,1,0:T(8,128)(2,1)S(1)}, ...), condition=%wide.region_11.12_spmd.clone, body=%wide.region_10.11_spmd.clone.sunk | while | flops 268959744 | bytes 4326479 | solution.py:71
  122.3 2.7 %convolution_add_fusion.2 = f32[2048,128]{1,0:T(8,128)S(1)} fusion(bf16[2,512,2048]{2,1,0:T(8,128)(2,1)} %get-tuple-element.384, s32[]{:T(128)} %get-tuple-element.376, f32[2048,128]{1,0:T(8,128)S(1)} %get-tuple-element.377, pred[]{:T(512)S(6)} %compare.7, bf16[2,512,128]{2,1,0:T(8,128)(2,1)S(1)} %get-tuple-element.385), kind=kOutput, calls=%fused_computation.18.clone.1 | convolution fusion | flops 268959744 | bytes 4326401 | tf_op jit(solution)/shard_map/while/body/eval_jaxpr/dot_general | solution.py:48
  125.0 2.6 %convolution_add_fusion.2 = f32[2048,128]{1,0:T(8,128)S(1)} fusion(bf16[2,512,2048]{2,1,0:T(8,128)(2,1)} %get-tuple-element.384, s32[]{:T(128)} %get-tuple-element.376, f32[2048,128]{1,0:T(8,128)S(1)} %get-tuple-element.377, pred[]{:T(512)S(6)} %compare.7, bf16[2,512,128]{2,1,0:T(8,128)(2,1)S(1)} %get-tuple-element.385), kind=kOutput, calls=%fused_computation.18.clone.1 | convolution fusion | flops 268959744 | bytes 4326401 | tf_op jit(solution)/shard_map/while/body/eval_jaxpr/dot_general | solution.py:48
  127.7 0.0 copy-start
  127.7 1.0 copy-done
  128.6 0.0 reduce-scatter.5.cloned.1.call-update
  128.7 0.0 copy-done.7
  128.7 0.6 dynamic-slice
  129.9 0.0 copy-done.5
  129.9 12.3 %all-reduce = f32[2048]{0:T(1024)S(1)} all-reduce(f32[2048]{0:T(1024)S(1)} %get-tuple-element.136), channel_id=4, replica_groups=mesh['groups'=2,'points'=4,'centers'=4] {'points'}, use_global_device_ids=true, to_apply=%region_9.10.clone | all-reduce | flops 2048 | bytes 16384
  142.3 0.1 dynamic-slice.1
  142.4 57.3 %reduce-scatter.3.cloned.1.call-done = f32[512,512]{1,0:T(8,128)} async-done(((f32[2048,512]{1,0:T(8,128)}), f32[512,512]{1,0:T(8,128)}) %reduce-scatter.3.cloned.1.call-update) | async-done | bytes 1048592 | tf_op jit(solution)/shard_map/reduce_scatter | solution.py:84
  199.6 0.0 copy-done.2
  199.6 2.4 %subtract_multiply_fusion = f32[512,512]{1,0:T(8,128)} fusion(f32[512,512]{1,0:T(8,128)} %reduce-scatter.3.cloned.1.call-done, bf16[512,512]{1,0:T(8,128)(2,1)S(1)} %copy-done.2, f32[512]{0:T(512)S(1)} %dynamic-slice.1, f32[512]{0:T(512)S(1)} %convert_multiply_fusion.1), kind=kLoop, calls=%fused_computation.25 | loop fusion | flops 1048576 | bytes 2625536 | tf_op jit(solution)/shard_map/mul | solution.py:88
  202.1 28.1 %reduce-scatter.5.cloned.1.call-done = f32[512,128]{1,0:T(8,128)} async-done(((f32[2048,128]{1,0:T(8,128)}), f32[512,128]{1,0:T(8,128)}) %reduce-scatter.5.cloned.1.call-update) | async-done | bytes 262160 | tf_op jit(solution)/shard_map/reduce_scatter | solution.py:72
  (8 shorter events, 0.0 us)
Async XLA Ops:
  7.2 59.4 %all-gather.5.cloned.1.call-start = ((), (), s32[]{:S(2)}) async-start(), calls=%async_computation.2 | async-start | bytes 2621440 | tf_op jit(solution)/shard_map/all_gather | solution.py:16
  7.9 98.6 %all-gather.7.cloned.1.call-start = ((), (), s32[]{:S(2)}) async-start(), calls=%async_computation.5 | async-start | bytes 2621440 | tf_op jit(solution)/shard_map/all_gather | solution.py:9
  80.5 27.8 %copy-start.3 = (f32[1024,128]{1,0:T(8,128)S(1)}, f32[1024,128]{1,0:T(8,128)}, u32[]{:S(2)}) copy-start(f32[1024,128]{1,0:T(8,128)} %param.15) | copy-start | bytes 1572868
  80.5 27.8 %copy-start.4 = (f32[1024,128]{1,0:T(8,128)S(1)}, f32[1024,128]{1,0:T(8,128)}, u32[]{:S(2)}) copy-start(f32[1024,128]{1,0:T(8,128)} %param.14) | copy-start | bytes 1572868
  80.5 27.8 %copy-start.6 = (f32[128]{0:T(128)S(1)}, f32[128]{0:T(128)}, u32[]{:S(2)}) copy-start(f32[128]{0:T(128)} %param.16) | copy-start | bytes 1540
  80.5 28.0 %copy-start.1 = (bf16[2,512,512]{2,1,0:T(8,128)(2,1)S(1)}, bf16[2,512,512]{2,1,0:T(8,128)(2,1)}, u32[]{:S(2)}) copy-start(bf16[2,512,512]{2,1,0:T(8,128)(2,1)} %get-tuple-element.397) | copy-start | bytes 3145732
  85.0 114.7 %reduce-scatter.3.cloned.1.call-start = ((), (), s32[]{:S(2)}) async-start(), calls=%async_computation.3 | async-start | bytes 5242880 | tf_op jit(solution)/shard_map/reduce_scatter | solution.py:84
  122.2 108.0 %reduce-scatter.5.cloned.1.call-start = ((), (), s32[]{:S(2)}) async-start(), calls=%async_computation.4 | async-start | bytes 1310720 | tf_op jit(solution)/shard_map/reduce_scatter | solution.py:72
  122.3 6.4 %copy-start.7 = (u32[32]{0:T(128)S(1)}, u32[32]{0:T(128)}, u32[]{:S(2)}) copy-start(u32[32]{0:T(128)} %constant.66) | copy-start | bytes 388
  122.3 7.7 %copy-start.5 = (bf16[512]{0:T(512)(128)(2,1)S(1)}, bf16[512]{0:T(512)(128)(2,1)}, u32[]{:S(2)}) copy-start(bf16[512]{0:T(512)(128)(2,1)} %param.19) | copy-start | bytes 3076
  122.3 77.4 %copy-start.2 = (bf16[512,512]{1,0:T(8,128)(2,1)S(1)}, bf16[512,512]{1,0:T(8,128)(2,1)}, u32[]{:S(2)}) copy-start(bf16[512,512]{1,0:T(8,128)(2,1)} %param.17) | copy-start | bytes 1572868
  127.7 1.0 copy-start
Sparse Core Ops, SparseCore 0:
  9.6 56.9 all-gather.4
  85.1 21.3 all-gather.6
  122.3 77.2 reduce-scatter.2
  202.5 27.6 reduce-scatter.4
